TPU v7x, 256 devices: a whole 4x4x8 slice. The times are simulated.
256 devices in a mesh: row: 8 (over z), col: 32 (over y, x, core).
Axes of the slice: x: 4, y: 4, z: 8, core: 2. Of those that a mesh axis runs over, the one named last changes fastest.
Arguments:
- panel_block: bfloat16 [28672, 1024], P(('row', 'col')), may hold values from -1.5 to 1.5
- diag_inverse: bfloat16 [2, 512, 512], replicated
- trailing: bfloat16 [28672, 28672], P('row', 'col'), may hold values from -6 to 6
Outputs:
- factor_panel: bfloat16 [28672, 1024], P(('row', 'col'))
- updated: bfloat16 [28672, 28672], P('row', 'col')
All inputs are finite; a program needn't handle non-finite values.
Results may differ from a plain program's by a relative error of at most 0.0054.
Values may be sent and summed in bfloat16 or wider, within the bound.
A program may use at most 128 MiB of HBM per device.

v0:
```python
import jax
import jax.numpy as jnp
from jax import lax
from jax.sharding import PartitionSpec as P

NB = 512
PANELS = 2


def sent_to_all(x, axis):
    peers = lax.axis_size(axis)
    return lax.all_to_all(jnp.broadcast_to(x[None], (peers, *x.shape)), axis, 0, 0, tiled=True)


def laid_out(pieces, dim):
    pieces = jnp.moveaxis(pieces, 0, dim)
    dims = pieces.shape
    return pieces.reshape(*dims[:dim], dims[dim] * dims[dim + 1], *dims[dim + 2 :])


def collect(x, axis, dim):
    pieces = sent_to_all(x, axis)
    return laid_out(pieces, dim)


def body(panel_block, diag_inverse, trailing):
    pieces = []
    for panel in range(PANELS):
        columns = panel_block[:, panel * NB : (panel + 1) * NB]
        pieces.append(
            jnp.dot(
                columns, jnp.tril(diag_inverse[panel]).T, preferred_element_type=jnp.float32
            ).astype(jnp.bfloat16)
        )
    factor = jnp.concatenate(pieces, axis=1)
    row_block = lax.all_gather(factor, "col", axis=0, tiled=True)
    product = lax.dot_general(
        row_block,
        collect(factor, "row", 0),
        (((1,), (1,)), ((), ())),
        preferred_element_type=jnp.float32,
    )
    updated = (trailing.astype(jnp.float32) - product).astype(jnp.bfloat16)
    return (factor, updated)


def solution(mesh):
    placed = (P(("row", "col"), None), P(), P("row", "col"))
    return jax.shard_map(
        body,
        mesh=mesh,
        in_specs=placed,
        out_specs=(P(("row", "col"), None), P("row", "col")),
        check_vma=False,
    )
```

profile of v0, /device:TPU:1, one launch (start us, length us, event | category | flops | bytes accessed | tf_op | source)
XLA Modules:
  0.0 91.9 jit_solution(386972775527290636)
XLA Ops:
  7.2 0.0 all-gather.2.cloned.1.call-start
  7.2 1.3 %fusion.1 = bf16[112,512]{1,0:T(8,128)(2,1)S(1)} fusion(bf16[2,512,512]{2,1,0:T(8,128)(2,1)} %param.4, bf16[112,1024]{1,0:T(8,128)(2,1)} %param.3), kind=kOutput, calls=%fused_computation.4 | convolution fusion | flops 59301888 | bytes 753664 | tf_op jit(solution)/shard_map/dot_general | solution.py:31
  8.6 1.3 %fusion = bf16[112,512]{1,0:T(8,128)(2,1)S(1)} fusion(bf16[2,512,512]{2,1,0:T(8,128)(2,1)} %param.4, bf16[112,1024]{1,0:T(8,128)(2,1)} %param.3), kind=kOutput, calls=%fused_computation.3 | convolution fusion | flops 59301888 | bytes 753664 | tf_op jit(solution)/shard_map/dot_general | solution.py:31
  9.9 0.7 pad_maximum_fusion
  10.6 0.0 all-gather.2.cloned.1.call-update
  10.6 1.2 %broadcast_in_dim.12 = bf16[8,112,1024]{2,1,0:T(8,128)(2,1)S(1)} broadcast(bf16[112,1024]{1,0:T(8,128)(2,1)} %pad_maximum_fusion), dimensions={1,2} | broadcast | bytes 2064384 | tf_op jit(solution)/shard_map/broadcast_in_dim | solution.py:12
  11.8 52.9 %all_to_all.5 = bf16[8,112,1024]{2,1,0:T(8,128)(2,1)S(1)} all-to-all(bf16[8,112,1024]{2,1,0:T(8,128)(2,1)S(1)} %broadcast_in_dim.12), channel_id=1, replica_groups=mesh['row'=8,'col'=32] {'row'}, dimensions={0} | all-to-all | bytes 3670016 | tf_op jit(solution)/shard_map/all_to_all | solution.py:12
  64.7 6.6 %all-gather.2.cloned.1.call-done = bf16[3584,1024]{1,0:T(8,128)(2,1)} async-done(((bf16[112,1024]{1,0:T(8,128)(2,1)}), bf16[3584,1024]{1,0:T(8,128)(2,1)}) %all-gather.2.cloned.1.call-update) | async-done | bytes 7340048 | tf_op jit(solution)/shard_map/all_gather | solution.py:36
  71.3 13.8 %subtract_convert_fusion = bf16[3584,896]{1,0:T(8,128)(2,1)} fusion(bf16[3584,896]{1,0:T(8,128)(2,1)} %param.5, bf16[3584,1024]{1,0:T(8,128)(2,1)} %all-gather.2.cloned.1.call-done, bf16[896,1024]{1,0:T(8,128)(2,1)S(1)} %bitcast.17), kind=kOutput, calls=%fused_computation | convolution fusion | flops 6586302464 | bytes 22020096 | tf_op jit(solution)/shard_map/dot_general | solution.py:37
Async XLA Ops:
  7.2 64.1 %all-gather.2.cloned.1.call-start = ((), (), s32[]{:S(2)}) async-start(), calls=%async_computation.1 | async-start | bytes 7569408 | tf_op jit(solution)/shard_map/all_gather | solution.py:36
Sparse Core Ops, SparseCore 0:
  11.1 60.0 all-gather.1
where the time goes:
time: 92.1 us; the launch traced here: 91.9 us
  blocking collectives  52.9 us (57%)
  matrix products  16.5 us (18%)
  between operations  14 us (15%)
  waiting for transfers between devices  6.57 us (7%)
  local copies, waits for them, and re-layouts  1.16 us (1%)
    all_to_all x1, blocking collectives, sent_to_all(): lax.all_to_all(jnp.broadcast_to(x[None], (peers, *x.shape)), axis, 0, 0,...  52.9 us
    dot_general x1, matrix products, body(): lax.dot_general(row_block, collect(factor, 'row', 0), (((1,), (1,)), ((),...  13.8 us
    all_gather x1, waiting for transfers between devices, body(): row_block = lax.all_gather(factor, 'col', axis=0, tiled=True)  6.55 us
    dot_general x2, matrix products, body(): jnp.dot(columns, jnp.tril(diag_inverse[panel]).T, preferred_element_type=...  2.68 us
  transfers between devices with their start and end apart: 1, of which 1 were waited for; matrix products, arithmetic and copies ran while one was open for 1% of the time, Pallas kernels for 0%

commit v1 on v0

v1 whole, which is shorter than its diff:
```python
import jax
import jax.numpy as jnp
from jax import lax
from jax.experimental import pallas as pl
from jax.experimental.pallas import tpu as pltpu
from jax.sharding import PartitionSpec as P

NB = 512
CH = 112
NZ = 8
NY = 4
NX = 4
PAIR = 2 * CH
COLS = NZ * CH
ROWS = NY * NX * PAIR
QUARTER = NB // 2
MESH = pl.DeviceIdType.MESH
NT = (((1,), (1,)), ((), ()))

RECV = [
    [(0, 0, -1), (1, -1, 0), (0, 0, 1), (1, 1, 0)],
    [(1, 0, -1), (0, -1, 0), (1, 0, 1), (0, 1, 0)],
    [(0, 0, 2), (1, 2, 0), (0, 1, -1), (1, -1, 1)],
    [(0, -1, -1), (1, -1, -1), (0, 1, 1), (1, 1, 1)],
    [(0, -1, 1), (1, 1, -1), (0, 1, 2), (1, 2, 1)],
    [(0, 2, 0), (1, 0, 2), (0, 2, -1), (1, -1, 2)],
    [(0, -1, 2), (1, 2, -1), (0, 2, 2), (1, 2, 2)],
    [(0, 2, 1), (1, 1, 2)],
]
ZPARTS = [(0, 0, NB), (1, 0, QUARTER), (1, QUARTER, QUARTER)]


def place():
    j = lax.axis_index("col")
    return lax.axis_index("row"), lax.div(j, 8), lax.rem(lax.div(j, 2), NX), lax.rem(j, 2)


def forwards(chunk):
    panel, dy, dx = chunk
    near, far = (dx, dy) if panel == 0 else (dy, dx)
    steps = []
    if far == 0:
        if near == 0:
            steps += [("near", 1), ("near", -1)]
        elif near == -1:
            steps += [("near", 1)]
        steps += [("far", 1), ("far", -1)]
    elif far == -1 and near in (0, 1):
        steps += [("far", 1)]
    elif far == 1 and near in (-1, 2):
        steps += [("far", -1)]
    axis = {"near": 1 - panel, "far": panel}
    return [(0, d) if axis[kind] == 1 else (d, 0) for kind, d in steps]


def gather_kernel(panel_hbm, diag_hbm, ra, rb, c0, c1, c2, pv, dv, lsem, ssem, rsem, zsem):
    z, y, x, c = place()
    sign = 1 - 2 * c
    rows = (ra, rb)
    cols = (c0, c1, c2)

    def device(dz, dy, dx, dc):
        zz = lax.rem(z + sign * dz + NZ, NZ)
        yy = lax.rem(y + sign * dy + NY, NY)
        xx = lax.rem(x + sign * dx + NX, NX)
        cc = 1 - c if dc else c
        return (zz, (yy * NX + xx) * 2 + cc)

    loads = [
        pltpu.make_async_copy(panel_hbm, pv, lsem.at[0]),
        pltpu.make_async_copy(diag_hbm, dv, lsem.at[1]),
    ]
    for load in loads:
        load.start()
    barrier = pltpu.get_barrier_semaphore()
    around = [(1, 0, 0, 0), (-1, 0, 0, 0), (0, 1, 0, 0), (0, -1, 0, 0), (0, 0, 1, 0), (0, 0, -1, 0), (0, 0, 0, 1)]
    for offset in around:
        pl.semaphore_signal(barrier, inc=1, device_id=device(*offset), device_id_type=MESH)
    for load in loads:
        load.wait()

    mine = pl.ds(pl.multiple_of(c * CH, 16), CH)
    own = pl.ds(pl.multiple_of(z * CH, 16), CH)
    below = lax.broadcasted_iota(jnp.int32, (NB, NB), 0) >= lax.broadcasted_iota(jnp.int32, (NB, NB), 1)
    for panel in range(2):
        full = dv[panel].astype(jnp.float32)
        lower = jnp.where(below, full, 0.0).astype(jnp.bfloat16)
        block = lax.dot_general(
            pv[:, panel * NB : (panel + 1) * NB], lower, NT, preferred_element_type=jnp.float32
        ).astype(jnp.bfloat16)
        rows[panel][y, x, mine, :] = block
        for part, (of, first, width) in enumerate(ZPARTS):
            if of == panel:
                cols[part][own, :] = block[:, first : first + width]
    pl.semaphore_wait(barrier, len(around))

    sent = []

    def send(ref, recv_sem, offset):
        copy = pltpu.make_async_remote_copy(
            src_ref=ref,
            dst_ref=ref,
            send_sem=ssem.at[len(sent)],
            recv_sem=recv_sem,
            device_id=device(*offset),
            device_id_type=MESH,
        )
        copy.start()
        sent.append(copy)

    def slot(chunk, mirrored=False):
        panel, dy, dx = chunk
        way, core = (-sign, 1 - c) if mirrored else (sign, c)
        yy = lax.rem(y + way * dy + NY, NY)
        xx = lax.rem(x + way * dx + NX, NX)
        ref = rows[panel].at[yy, xx, pl.ds(pl.multiple_of(core * CH, 16), CH), :]
        return ref, rsem.at[panel * 32 + (yy * NX + xx) * 2 + core]

    def wait(ref, sem):
        pltpu.make_async_remote_copy(
            src_ref=ref, dst_ref=ref, send_sem=ssem.at[0], recv_sem=sem, device_id=device(0, 0, 0, 1), device_id_type=MESH
        ).wait_recv()

    def pass_on(chunk):
        ref, sem = slot(chunk)
        for dy, dx in forwards(chunk):
            send(ref, sem, (0, dy, dx, 0))
        send(ref, sem, (0, 0, 0, 1))

    def zslot(part, dz):
        zz = lax.rem(z + sign * dz + NZ, NZ)
        return cols[part].at[pl.ds(pl.multiple_of(zz * CH, 16), CH), :], zsem.at[part * NZ + zz]

    def zsend(part, dz, way):
        ref, sem = zslot(part, dz)
        send(ref, sem, (way, 0, 0, 0))

    def zround(part, hop):
        for way in (1, -1):
            if hop == NZ // 2 and way != (1 if part == 0 else -1):
                continue
            ref, sem = zslot(part, -way * hop)
            wait(ref, sem)
            if hop + 1 < NZ // 2 or (hop + 1 == NZ // 2 and way == (1 if part == 0 else -1)):
                send(ref, sem, (way, 0, 0, 0))

    zorder = [(part, hop) for hop in range(1, NZ // 2 + 1) for part in range(len(ZPARTS))]
    for part in range(len(ZPARTS)):
        if part == 0:
            pass_on((0, 0, 0))
        if part == 1:
            pass_on((1, 0, 0))
        for way in (1, -1):
            zsend(part, 0, way)
    done = 0
    for step, chunks in enumerate(RECV):
        for chunk in chunks:
            wait(*slot(chunk))
            pass_on(chunk)
        upto = ZSTEPS[step]
        for part, hop in zorder[done:upto]:
            zround(part, hop)
        done = upto
    for chunks in [[(0, 0, 0), (1, 0, 0)]] + RECV:
        for chunk in chunks:
            wait(*slot(chunk, mirrored=True))
    for copy in sent:
        copy.wait_send()


ZSTEPS = [1, 3, 4, 6, 7, 9, 12, 12]
N_SENDS = 30 + 32 + 7 * len(ZPARTS)
TILE = 448


def update_kernel(ra, rb, c0, c1, c2, t_hbm, f_hbm, o_hbm, tb, ob, tsem, osem, fsem):
    _, y, x, c = place()
    mine = pl.ds(pl.multiple_of(c * CH, 16), CH)
    keep = [
        pltpu.make_async_copy(r.at[y, x, mine, :], f_hbm.at[:, panel * NB : (panel + 1) * NB], fsem.at[panel])
        for panel, r in enumerate((ra, rb))
    ]
    steps = ROWS // TILE
    pairs = TILE // PAIR

    def read(i, s):
        return pltpu.make_async_copy(t_hbm.at[pl.ds(pl.multiple_of(i * TILE, 64), TILE)], tb.at[s], tsem.at[s])

    def write(i, s):
        return pltpu.make_async_copy(ob.at[s], o_hbm.at[pl.ds(pl.multiple_of(i * TILE, 64), TILE)], osem.at[s])

    read(0, 0).start()
    read(1, 1).start()
    for copy in keep:
        copy.start()

    def step(i, _):
        s = lax.rem(i, 2)
        read(i, s).wait()
        yy = lax.div(i, NX // pairs)
        xx = pl.ds(lax.rem(i, NX // pairs) * pairs, pairs)
        left = ra[yy, xx].reshape(TILE, NB)
        right = rb[yy, xx].reshape(TILE, NB)
        product = lax.dot_general(left, c0[...], NT, preferred_element_type=jnp.float32)
        product += lax.dot_general(right[:, :QUARTER], c1[...], NT, preferred_element_type=jnp.float32)
        product += lax.dot_general(right[:, QUARTER:], c2[...], NT, preferred_element_type=jnp.float32)

        @pl.when(i >= 2)
        def _():
            write(i - 2, s).wait()

        ob[s] = (tb[s].astype(jnp.float32) - product).astype(jnp.bfloat16)
        write(i, s).start()

        @pl.when(i + 2 < steps)
        def _():
            read(i + 2, s).start()

        return 0

    lax.fori_loop(0, steps, step, 0)
    write(steps - 2, steps % 2).wait()
    write(steps - 1, (steps - 1) % 2).wait()
    for copy in keep:
        copy.wait()


def body(panel_block, diag_inverse, trailing):
    vmem = pl.BlockSpec(memory_space=pltpu.VMEM)
    hbm = pl.BlockSpec(memory_space=pltpu.HBM)
    bf16 = jnp.bfloat16
    half = jax.ShapeDtypeStruct((NY, NX, PAIR, NB), bf16)
    gathered = pl.pallas_call(
        gather_kernel,
        name="gather",
        out_shape=[half, half] + [jax.ShapeDtypeStruct((COLS, width), bf16) for _, _, width in ZPARTS],
        in_specs=[hbm] * 2,
        out_specs=[vmem] * (2 + len(ZPARTS)),
        scratch_shapes=[
            pltpu.VMEM((CH, 2 * NB), bf16),
            pltpu.VMEM((2, NB, NB), bf16),
            pltpu.SemaphoreType.DMA((2,)),
            pltpu.SemaphoreType.DMA((N_SENDS,)),
            pltpu.SemaphoreType.DMA((64,)),
            pltpu.SemaphoreType.DMA((NZ * len(ZPARTS),)),
        ],
        compiler_params=pltpu.CompilerParams(
            collective_id=0, has_side_effects=True, vmem_limit_bytes=24 << 20
        ),
    )(*(pltpu.with_memory_space_constraint(a, pltpu.HBM) for a in (panel_block, diag_inverse)))
    return pl.pallas_call(
        update_kernel,
        name="update",
        out_shape=[
            jax.ShapeDtypeStruct(panel_block.shape, bf16),
            jax.ShapeDtypeStruct(trailing.shape, bf16),
        ],
        in_specs=[vmem] * len(gathered) + [hbm],
        out_specs=[hbm] * 2,
        scratch_shapes=[
            pltpu.VMEM((2, TILE, COLS), bf16),
            pltpu.VMEM((2, TILE, COLS), bf16),
            pltpu.SemaphoreType.DMA((2,)),
            pltpu.SemaphoreType.DMA((2,)),
            pltpu.SemaphoreType.DMA((2,)),
        ],
        compiler_params=pltpu.CompilerParams(vmem_limit_bytes=24 << 20),
    )(*gathered, pltpu.with_memory_space_constraint(trailing, pltpu.HBM))


def solution(mesh):
    placed = (P(("row", "col"), None), P(), P("row", "col"))
    return jax.shard_map(
        body,
        mesh=mesh,
        in_specs=placed,
        out_specs=(P(("row", "col"), None), P("row", "col")),
        check_vma=False,
    )
```

time: 92.1 us -> 48.4 us (0.53)
  blocking collectives: 52.9 us -> 0 us
  Pallas kernels: 0 us -> 47.5 us
  matrix products: 16.5 us -> 0 us
  between operations: 14 us -> 0.64 us
  waiting for transfers between devices: 6.57 us -> 0 us
  local copies, waits for them, and re-layouts: 1.16 us -> 0 us
    all_to_all x1 -> x0, blocking collectives: 52.9 us -> none  [sent_to_all(): lax.all_to_all(jnp.broadcast_to(x[None], (peers, *x.shape)), axis, 0, 0,...]
    pallas_call x0 -> x2, Pallas kernels: none -> 47.5 us  [the longest x1 34.7 us: body(): pl.pallas_call(gather_kernel, name='gather', out_shape=[half, half] + [ja...]
    dot_general x3 -> x0, matrix products: 16.5 us -> none  [the longest x1 13.8 us: body(): lax.dot_general(row_block, collect(factor, 'row', 0), (((1,), (1,)), ((),...]
    all_gather x1 -> x0, waiting for transfers between devices: 6.55 us -> none  [body(): row_block = lax.all_gather(factor, 'col', axis=0, tiled=True)]
    broadcast_in_dim x1 -> x0, local copies, waits for them, and re-layouts: 1.16 us -> none  [sent_to_all(): jnp.broadcast_to(x[None], (peers, *x.shape))]
  transfers between devices with their start and end apart: 1 -> 0, of which waited for: 1 -> 0; matrix products, arithmetic and copies ran while one was open for 1% -> 0% of each run, Pallas kernels for 0% -> 0%
where the time goes in v1:
time: 48.4 us; the launch traced here: 48.2 us
  Pallas kernels  47.5 us (98%)
  between operations  0.64 us (1%)
    pallas_call x1, Pallas kernels, body(): pl.pallas_call(gather_kernel, name='gather', out_shape=[half, half] + [ja...  34.7 us
    pallas_call x1, Pallas kernels, body(): pl.pallas_call(update_kernel, name='update', out_shape=[jax.ShapeDtypeStr...  12.8 us

profile of v1, /device:TPU:1, one launch (start us, length us, event | category | flops | bytes accessed | tf_op | source)
XLA Modules:
  0.0 48.2 jit_solution(1247751325185622264)
XLA Ops:
  0.6 34.7 %gather.1 = (bf16[4,4,224,512]{3,2,1,0:T(8,128)(2,1)S(1)}, bf16[4,4,224,512]{3,2,1,0:T(8,128)(2,1)S(1)}, bf16[896,512]{1,0:T(8,128)(2,1)S(1)}, bf16[896,256]{1,0:T(8,128)(2,1)S(1)}, bf16[896,256]{1,0:T(8,128)(2,1)S(1)}) custom-call(bf16[112,1024]{1,0:T(8,128)(2,1)} %panel_hbm.1, bf16[2,512,512]{2,1,0:T(8,128)(2,1)} %diag_hbm.1), custom_call_target="tpu_custom_call" | custom-call | tf_op jit(solution)/shard_map/gather/pallas_call | solution.py:233
  35.3 12.8 %update.1 = (bf16[112,1024]{1,0:T(8,128)(2,1)}, bf16[3584,896]{1,0:T(8,128)(2,1)}) custom-call(bf16[4,4,224,512]{3,2,1,0:T(8,128)(2,1)S(1)} %get-tuple-element.7.ra, bf16[4,4,224,512]{3,2,1,0:T(8,128)(2,1)S(1)} %get-tuple-element.8.rb, bf16[896,512]{1,0:T(8,128)(2,1)S(1)} %get-tuple-element.9.c0, bf16[896,256]{1,0:T(8,128)(2,1)S(1)} %get-tuple-element.10.c1, ...), custom_call_target="tpu_custom_call" | custom-call | tf_op jit(solution)/shard_map/update/pallas_call | solution.py:251

commit v2 on v1

v2 whole, which is shorter than its diff:
```python
import jax
import jax.numpy as jnp
from jax import lax
from jax.experimental import pallas as pl
from jax.experimental.pallas import tpu as pltpu
from jax.sharding import PartitionSpec as P

NB = 512
CH = 112
NZ = 8
NY = 4
NX = 4
PAIR = 2 * CH
COLS = NZ * CH
ROWS = NY * NX * PAIR
QUARTER = NB // 2
MESH = pl.DeviceIdType.MESH
NT = (((1,), (1,)), ((), ()))

RECV = [
    [(0, 0, -1), (1, -1, 0), (0, 0, 1), (1, 1, 0)],
    [(1, 0, -1), (0, -1, 0), (1, 0, 1), (0, 1, 0)],
    [(0, 0, 2), (1, 2, 0), (0, 1, -1), (1, -1, 1)],
    [(0, -1, -1), (1, -1, -1), (0, 1, 1), (1, 1, 1)],
    [(0, -1, 1), (1, 1, -1), (0, 1, 2), (1, 2, 1)],
    [(0, 2, 0), (1, 0, 2), (0, 2, -1), (1, -1, 2)],
    [(0, -1, 2), (1, 2, -1), (0, 2, 2), (1, 2, 2)],
    [(0, 2, 1), (1, 1, 2)],
]
ZPARTS = [(0, 0), (0, QUARTER), (1, 0), (1, QUARTER)]
PLAN = [
    ("own", 3),
    ("z", 0, 1),
    ("z", 1, 1),
    ("row", 0),
    ("z", 2, 1),
    ("z", 3, 1),
    ("row", 1),
    ("z", 0, 2),
    ("z", 1, 2),
    ("row", 2),
    ("z", 2, 2),
    ("z", 3, 2),
    ("row", 3),
    ("z", 0, 3),
    ("z", 1, 3),
    ("row", 4),
    ("z", 2, 3),
    ("z", 3, 3),
    ("row", 5),
    ("z", 0, 4),
    ("z", 1, 4),
    ("do", 0, [(0, -1), (0, 0), (0, 1), (0, 2)]),
    ("row", 6),
    ("do", 0, [(1, -1), (1, 0), (1, 1)]),
    ("do", 0, [(-1, -1), (-1, 0), (-1, 1)]),
    ("z", 2, 4),
    ("z", 3, 4),
    ("row", 7),
    ("do", 0, [(1, 2), (-1, 2), (2, 0), (2, 2)]),
    ("do", 1, [(-1, 0), (0, 0), (1, 0), (2, 0)]),
    ("do", 1, [(-1, -1), (0, -1), (1, -1)]),
    ("do", 1, [(-1, 1), (0, 1), (1, 1)]),
]
DONE = {(step[1], chip) for step in PLAN if step[0] == "do" for chip in step[2]}
CHIPS = [(dy, dx) for dy in (2, -1, 0, 1) for dx in (-1, 1, 0, 2)]
UNTOUCHED = [chip for chip in CHIPS if (0, chip) not in DONE and (1, chip) not in DONE]


def place():
    j = lax.axis_index("col")
    return lax.axis_index("row"), lax.div(j, 8), lax.rem(lax.div(j, 2), NX), lax.rem(j, 2)


def forwards(chunk):
    panel, dy, dx = chunk
    near, far = (dx, dy) if panel == 0 else (dy, dx)
    steps = []
    if far == 0:
        if near == 0:
            steps += [("near", 1), ("near", -1)]
        elif near == -1:
            steps += [("near", 1)]
        steps += [("far", 1), ("far", -1)]
    elif far == -1 and near in (0, 1):
        steps += [("far", 1)]
    elif far == 1 and near in (-1, 2):
        steps += [("far", -1)]
    axis = {"near": 1 - panel, "far": panel}
    return [(0, d) if axis[kind] == 1 else (d, 0) for kind, d in steps]


def gather_kernel(panel_hbm, diag_hbm, t_hbm, ra, rb, ca, cb, acc, pv, dv, tv, lsem, ssem, rsem, zsem):
    z, y, x, c = place()
    sign = 1 - 2 * c
    rows = (ra, rb)
    cols = (ca, cb)

    def device(dz, dy, dx, dc):
        zz = lax.rem(z + sign * dz + NZ, NZ)
        yy = lax.rem(y + sign * dy + NY, NY)
        xx = lax.rem(x + sign * dx + NX, NX)
        cc = 1 - c if dc else c
        return (zz, (yy * NX + xx) * 2 + cc)

    loads = [
        pltpu.make_async_copy(panel_hbm, pv, lsem.at[0]),
        pltpu.make_async_copy(diag_hbm.at[0], dv.at[0], lsem.at[1]),
        pltpu.make_async_copy(diag_hbm.at[1], dv.at[1], lsem.at[2]),
        pltpu.make_async_copy(t_hbm, tv, lsem.at[3]),
    ]
    for load in loads[:3]:
        load.start()
    barrier = pltpu.get_barrier_semaphore()
    around = [(1, 0, 0, 0), (-1, 0, 0, 0), (0, 1, 0, 0), (0, -1, 0, 0), (0, 0, 1, 0), (0, 0, -1, 0), (0, 0, 0, 1)]
    for offset in around:
        pl.semaphore_signal(barrier, inc=1, device_id=device(*offset), device_id_type=MESH)

    mine = pl.ds(pl.multiple_of(c * CH, 16), CH)
    own = pl.ds(pl.multiple_of(z * CH, 16), CH)
    below = lax.broadcasted_iota(jnp.int32, (NB, NB), 0) >= lax.broadcasted_iota(jnp.int32, (NB, NB), 1)

    def factor(panel):
        full = dv[panel].astype(jnp.float32)
        lower = jnp.where(below, full, 0.0).astype(jnp.bfloat16)
        block = lax.dot_general(
            pv[:, panel * NB : (panel + 1) * NB], lower, NT, preferred_element_type=jnp.float32
        ).astype(jnp.bfloat16)
        rows[panel][y, x, mine, :] = block
        cols[panel][own, :] = block

    sent = []

    def send(ref, recv_sem, offset):
        copy = pltpu.make_async_remote_copy(
            src_ref=ref,
            dst_ref=ref,
            send_sem=ssem.at[len(sent)],
            recv_sem=recv_sem,
            device_id=device(*offset),
            device_id_type=MESH,
        )
        copy.start()
        sent.append(copy)

    def slot(chunk, mirrored=False):
        panel, dy, dx = chunk
        way, core = (-sign, 1 - c) if mirrored else (sign, c)
        yy = lax.rem(y + way * dy + NY, NY)
        xx = lax.rem(x + way * dx + NX, NX)
        ref = rows[panel].at[yy, xx, pl.ds(pl.multiple_of(core * CH, 16), CH), :]
        return ref, rsem.at[panel * 32 + (yy * NX + xx) * 2 + core]

    def wait(ref, sem):
        pltpu.make_async_remote_copy(
            src_ref=ref, dst_ref=ref, send_sem=ssem.at[0], recv_sem=sem, device_id=device(0, 0, 0, 1), device_id_type=MESH
        ).wait_recv()

    def pass_on(chunk):
        ref, sem = slot(chunk)
        for dy, dx in forwards(chunk):
            send(ref, sem, (0, dy, dx, 0))
        send(ref, sem, (0, 0, 0, 1))

    def zslot(part, dz):
        panel, first = ZPARTS[part]
        zz = lax.rem(z + sign * dz + NZ, NZ)
        ref = cols[panel].at[pl.ds(pl.multiple_of(zz * CH, 16), CH), pl.ds(first, QUARTER)]
        return ref, zsem.at[part * NZ + zz]

    def zstart(part):
        ref, sem = zslot(part, 0)
        for way in (1, -1):
            send(ref, sem, (way, 0, 0, 0))

    def zpass_on(part, hop):
        last_way = 1 if part % 2 == 0 else -1
        for way in (1, -1):
            if hop == NZ // 2 and way != last_way:
                continue
            ref, sem = zslot(part, -way * hop)
            wait(ref, sem)
            if hop + 1 < NZ // 2 or (hop + 1 == NZ // 2 and way == last_way):
                send(ref, sem, (way, 0, 0, 0))

    from_sibling = set()

    def wait_sibling(chunk):
        if chunk not in from_sibling:
            from_sibling.add(chunk)
            wait(*slot(chunk, mirrored=True))

    def other(d):
        return d if d == 2 else -d

    touched = set()

    def chip_at(dy, dx):
        return lax.rem(y + sign * dy + NY, NY), lax.rem(x + sign * dx + NX, NX)

    def update(panel, chips):
        for dy, dx in chips:
            wait_sibling((panel, other(dy), other(dx)))
        for dy, dx in chips:
            yy, xx = chip_at(dy, dx)
            product = lax.dot_general(rows[panel][yy, xx], cols[panel][...], NT, preferred_element_type=jnp.float32)
            before = acc[yy, xx] if (dy, dx) in touched else tv[yy, xx].astype(jnp.float32)
            touched.add((dy, dx))
            acc[yy, xx] = before - product

    loads[0].wait()
    loads[1].wait()
    factor(0)
    pl.semaphore_wait(barrier, len(around))
    pass_on((0, 0, 0))
    zstart(0)
    zstart(1)
    loads[2].wait()
    factor(1)
    pass_on((1, 0, 0))
    zstart(2)
    loads[3].start()
    for what, *arg in PLAN:
        if what == "row":
            for chunk in RECV[arg[0]]:
                wait(*slot(chunk))
                pass_on(chunk)
            if arg[0] == 3:
                loads[3].wait()
                for chip in UNTOUCHED:
                    yy, xx = chip_at(*chip)
                    acc[yy, xx] = tv[yy, xx].astype(jnp.float32)
        elif what == "z":
            zpass_on(*arg)
        elif what == "own":
            zstart(*arg)
        else:
            update(*arg)
    for chunks in [[(0, 0, 0), (1, 0, 0)]] + RECV:
        for chunk in chunks:
            wait_sibling(chunk)
    for copy in sent:
        copy.wait_send()


N_SENDS = 30 + 32 + 7 * len(ZPARTS)


def update_kernel(ra, rb, ca, cb, acc, f_hbm, o_hbm, ob, osem, fsem):
    _, y, x, c = place()
    sign = 1 - 2 * c
    mine = pl.ds(pl.multiple_of(c * CH, 16), CH)
    keep = [
        pltpu.make_async_copy(r.at[y, x, mine, :], f_hbm.at[:, panel * NB : (panel + 1) * NB], fsem.at[panel])
        for panel, r in enumerate((ra, rb))
    ]
    for copy in keep:
        copy.start()

    writes = []
    for i, (dy, dx) in enumerate(CHIPS):
        yy = lax.rem(y + sign * dy + NY, NY)
        xx = lax.rem(x + sign * dx + NX, NX)
        value = acc[yy, xx]
        for panel, (r, cf) in enumerate(((ra, ca), (rb, cb))):
            if (panel, (dy, dx)) not in DONE:
                value -= lax.dot_general(r[yy, xx], cf[...], NT, preferred_element_type=jnp.float32)
        ob[i] = value.astype(jnp.bfloat16)
        copy = pltpu.make_async_copy(ob.at[i], o_hbm.at[yy, xx], osem.at[i])
        copy.start()
        writes.append(copy)
    for copy in writes:
        copy.wait()
    for copy in keep:
        copy.wait()


def body(panel_block, diag_inverse, trailing):
    vmem = pl.BlockSpec(memory_space=pltpu.VMEM)
    hbm = pl.BlockSpec(memory_space=pltpu.HBM)
    bf16 = jnp.bfloat16
    half = jax.ShapeDtypeStruct((NY, NX, PAIR, NB), bf16)
    column = jax.ShapeDtypeStruct((COLS, NB), bf16)
    blocks = (NY, NX, PAIR, COLS)
    inputs = (panel_block, diag_inverse, trailing.reshape(blocks))
    gathered = pl.pallas_call(
        gather_kernel,
        name="gather",
        out_shape=[half, half, column, column, jax.ShapeDtypeStruct(blocks, jnp.float32)],
        in_specs=[hbm] * 3,
        out_specs=[vmem] * 5,
        scratch_shapes=[
            pltpu.VMEM((CH, 2 * NB), bf16),
            pltpu.VMEM((2, NB, NB), bf16),
            pltpu.VMEM(blocks, bf16),
            pltpu.SemaphoreType.DMA((4,)),
            pltpu.SemaphoreType.DMA((N_SENDS,)),
            pltpu.SemaphoreType.DMA((64,)),
            pltpu.SemaphoreType.DMA((NZ * len(ZPARTS),)),
        ],
        compiler_params=pltpu.CompilerParams(
            collective_id=0, has_side_effects=True, vmem_limit_bytes=24 << 20
        ),
    )(*(pltpu.with_memory_space_constraint(a, pltpu.HBM) for a in inputs))
    factor, updated = pl.pallas_call(
        update_kernel,
        name="update",
        out_shape=[
            jax.ShapeDtypeStruct(panel_block.shape, bf16),
            jax.ShapeDtypeStruct(blocks, bf16),
        ],
        in_specs=[vmem] * len(gathered),
        out_specs=[hbm] * 2,
        scratch_shapes=[
            pltpu.VMEM((NY * NX, PAIR, COLS), bf16),
            pltpu.SemaphoreType.DMA((NY * NX,)),
            pltpu.SemaphoreType.DMA((2,)),
        ],
        compiler_params=pltpu.CompilerParams(vmem_limit_bytes=24 << 20),
    )(*gathered)
    return factor, updated.reshape(trailing.shape)


def solution(mesh):
    placed = (P(("row", "col"), None), P(), P("row", "col"))
    return jax.shard_map(
        body,
        mesh=mesh,
        in_specs=placed,
        out_specs=(P(("row", "col"), None), P("row", "col")),
        check_vma=False,
    )
```

time: 48.4 us -> 42.8 us (0.88)
  Pallas kernels: 47.5 us -> 42 us
    pallas_call x1, Pallas kernels: 12.8 us -> 4.09 us  [body(): pl.pallas_call(update_kernel, name='update', out_shape=[jax.ShapeDtypeStr...]
    pallas_call x1, Pallas kernels: 34.7 us -> 37.9 us  [body(): pl.pallas_call(gather_kernel, name='gather', out_shape=[half, half, colum...]
where the time goes in v2:
time: 42.8 us; the launch traced here: 42.6 us
  Pallas kernels  42 us (98%)
  between operations  0.64 us (1%)
    pallas_call x1, Pallas kernels, body(): pl.pallas_call(gather_kernel, name='gather', out_shape=[half, half, colum...  37.9 us
    pallas_call x1, Pallas kernels, body(): pl.pallas_call(update_kernel, name='update', out_shape=[jax.ShapeDtypeStr...  4.09 us

profile of v2, /device:TPU:1, one launch (start us, length us, event | category | flops | bytes accessed | tf_op | source)
XLA Modules:
  0.0 42.6 jit_solution(7713044799045846053)
XLA Ops:
  0.6 37.9 %gather.1 = (bf16[4,4,224,512]{3,2,1,0:T(8,128)(2,1)S(1)}, bf16[4,4,224,512]{3,2,1,0:T(8,128)(2,1)S(1)}, bf16[896,512]{1,0:T(8,128)(2,1)S(1)}, bf16[896,512]{1,0:T(8,128)(2,1)S(1)}, f32[4,4,224,896]{3,2,1,0:T(8,128)S(1)}) custom-call(bf16[112,1024]{1,0:T(8,128)(2,1)} %panel_hbm.1, bf16[2,512,512]{2,1,0:T(8,128)(2,1)} %diag_hbm.1, ...), custom_call_target="tpu_custom_call" | custom-call | tf_op jit(solution)/shard_map/gather/pallas_call | solution.py:286
  38.6 4.1 %update.1 = (bf16[112,1024]{1,0:T(8,128)(2,1)}, bf16[4,4,224,896]{3,2,1,0:T(8,128)(2,1)}) custom-call(bf16[4,4,224,512]{3,2,1,0:T(8,128)(2,1)S(1)} %get-tuple-element.9.ra, bf16[4,4,224,512]{3,2,1,0:T(8,128)(2,1)S(1)} %get-tuple-element.10.rb, bf16[896,512]{1,0:T(8,128)(2,1)S(1)} %get-tuple-element.11.ca, bf16[896,512]{1,0:T(8,128)(2,1)S(1)} %get-tuple-element.12.cb, ...), custom_call_target="tpu_custom_call" | custom-call | tf_op jit(solution)/shard_map/update/pallas_call | solution.py:305

commit v3 on v2

--- a/solution.py
+++ b/solution.py
@@ -14,6 +14,8 @@
 COLS = NZ * CH
 ROWS = NY * NX * PAIR
 QUARTER = NB // 2
+LANES = 128
+TWO = 2 * LANES
 MESH = pl.DeviceIdType.MESH
 NT = (((1,), (1,)), ((), ()))
 
@@ -28,6 +30,9 @@
     [(0, 2, 1), (1, 1, 2)],
 ]
 ZPARTS = [(0, 0), (0, QUARTER), (1, 0), (1, QUARTER)]
+CROSS = [(0, 0), (0, -1), (0, 1), (-1, 0), (1, 0)]
+CORNERS = [(1, -1), (1, 1), (-1, -1), (-1, 1)]
+ENDS = [(0, 2), (2, 0)]
 PLAN = [
     ("own", 3),
     ("z", 0, 1),
@@ -36,35 +41,40 @@
     ("z", 2, 1),
     ("z", 3, 1),
     ("row", 1),
+    ("do", 1, CROSS),
     ("z", 0, 2),
     ("z", 1, 2),
     ("row", 2),
     ("z", 2, 2),
     ("z", 3, 2),
     ("row", 3),
+    ("do", 2, CROSS),
     ("z", 0, 3),
     ("z", 1, 3),
     ("row", 4),
+    ("do", 1, CORNERS),
     ("z", 2, 3),
     ("z", 3, 3),
+    ("do", 2, CORNERS),
     ("row", 5),
+    ("do", 3, CROSS),
+    ("do", 1, ENDS),
+    ("do", 2, ENDS),
     ("z", 0, 4),
     ("z", 1, 4),
-    ("do", 0, [(0, -1), (0, 0), (0, 1), (0, 2)]),
+    ("do", 3, CORNERS),
     ("row", 6),
-    ("do", 0, [(1, -1), (1, 0), (1, 1)]),
-    ("do", 0, [(-1, -1), (-1, 0), (-1, 1)]),
     ("z", 2, 4),
     ("z", 3, 4),
+    ("do", 4, CROSS),
     ("row", 7),
-    ("do", 0, [(1, 2), (-1, 2), (2, 0), (2, 2)]),
-    ("do", 1, [(-1, 0), (0, 0), (1, 0), (2, 0)]),
-    ("do", 1, [(-1, -1), (0, -1), (1, -1)]),
-    ("do", 1, [(-1, 1), (0, 1), (1, 1)]),
+    ("do", 3, ENDS),
+    ("do", 4, CORNERS),
+    ("do", 4, ENDS),
 ]
-DONE = {(step[1], chip) for step in PLAN if step[0] == "do" for chip in step[2]}
-CHIPS = [(dy, dx) for dy in (2, -1, 0, 1) for dx in (-1, 1, 0, 2)]
-UNTOUCHED = [chip for chip in CHIPS if (0, chip) not in DONE and (1, chip) not in DONE]
+READY = CROSS + CORNERS + ENDS
+OPEN = [(dy, dx) for dy in (2, -1, 1, 0) for dx in (2, -1, 1, 0) if (dy, dx) not in READY]
+CHIPS = [chip for k, first in enumerate(OPEN) for chip in [first, *READY[2 * k : 2 * k + 2]]] + READY[2 * len(OPEN) :]
 
 
 def place():
@@ -90,7 +100,7 @@
     return [(0, d) if axis[kind] == 1 else (d, 0) for kind, d in steps]
 
 
-def gather_kernel(panel_hbm, diag_hbm, t_hbm, ra, rb, ca, cb, acc, pv, dv, tv, lsem, ssem, rsem, zsem):
+def gather_kernel(panel_hbm, diag_hbm, t_hbm, ra, rb, ca, cb, acc, tv, pv, dv, lsem, ssem, rsem, zsem):
     z, y, x, c = place()
     sign = 1 - 2 * c
     rows = (ra, rb)
@@ -117,7 +127,10 @@
         pl.semaphore_signal(barrier, inc=1, device_id=device(*offset), device_id_type=MESH)
 
     mine = pl.ds(pl.multiple_of(c * CH, 16), CH)
-    own = pl.ds(pl.multiple_of(z * CH, 16), CH)
+    own = pl.ds(pl.multiple_of(z * LANES, LANES), CH)
+    for cf in cols:
+        for k in range(NZ):
+            cf[k * LANES + CH : (k + 1) * LANES, :] = jnp.zeros((LANES - CH, NB), jnp.bfloat16)
     below = lax.broadcasted_iota(jnp.int32, (NB, NB), 0) >= lax.broadcasted_iota(jnp.int32, (NB, NB), 1)
 
     def factor(panel):
@@ -165,7 +178,7 @@
     def zslot(part, dz):
         panel, first = ZPARTS[part]
         zz = lax.rem(z + sign * dz + NZ, NZ)
-        ref = cols[panel].at[pl.ds(pl.multiple_of(zz * CH, 16), CH), pl.ds(first, QUARTER)]
+        ref = cols[panel].at[pl.ds(pl.multiple_of(zz * LANES, LANES), CH), pl.ds(first, QUARTER)]
         return ref, zsem.at[part * NZ + zz]
 
     def zstart(part):
@@ -193,20 +206,19 @@
     def other(d):
         return d if d == 2 else -d
 
-    touched = set()
-
-    def chip_at(dy, dx):
-        return lax.rem(y + sign * dy + NY, NY), lax.rem(x + sign * dx + NX, NX)
-
-    def update(panel, chips):
+    def update(hops, chips):
+        side = 1 - 2 * lax.rem(z, 2)
+        at = lax.rem(z + side * (hops if hops % 2 == 1 else -hops) + NZ, NZ)
+        lanes = pl.ds(pl.multiple_of(lax.div(at, 2) * TWO, TWO), TWO)
         for dy, dx in chips:
-            wait_sibling((panel, other(dy), other(dx)))
+            for panel in range(2):
+                wait_sibling((panel, other(dy), other(dx)))
         for dy, dx in chips:
-            yy, xx = chip_at(dy, dx)
-            product = lax.dot_general(rows[panel][yy, xx], cols[panel][...], NT, preferred_element_type=jnp.float32)
-            before = acc[yy, xx] if (dy, dx) in touched else tv[yy, xx].astype(jnp.float32)
-            touched.add((dy, dx))
-            acc[yy, xx] = before - product
+            yy = lax.rem(y + sign * dy + NY, NY)
+            xx = lax.rem(x + sign * dx + NX, NX)
+            product = lax.dot_general(ra[yy, xx], ca[lanes, :], NT, preferred_element_type=jnp.float32)
+            product += lax.dot_general(rb[yy, xx], cb[lanes, :], NT, preferred_element_type=jnp.float32)
+            acc[yy, xx, :, lanes] = product
 
     loads[0].wait()
     loads[1].wait()
@@ -225,11 +237,6 @@
             for chunk in RECV[arg[0]]:
                 wait(*slot(chunk))
                 pass_on(chunk)
-            if arg[0] == 3:
-                loads[3].wait()
-                for chip in UNTOUCHED:
-                    yy, xx = chip_at(*chip)
-                    acc[yy, xx] = tv[yy, xx].astype(jnp.float32)
         elif what == "z":
             zpass_on(*arg)
         elif what == "own":
@@ -241,12 +248,13 @@
             wait_sibling(chunk)
     for copy in sent:
         copy.wait_send()
+    loads[3].wait()
 
 
 N_SENDS = 30 + 32 + 7 * len(ZPARTS)
 
 
-def update_kernel(ra, rb, ca, cb, acc, f_hbm, o_hbm, ob, osem, fsem):
+def update_kernel(ra, rb, ca, cb, acc, tv, f_hbm, o_hbm, ob, osem, fsem):
     _, y, x, c = place()
     sign = 1 - 2 * c
     mine = pl.ds(pl.multiple_of(c * CH, 16), CH)
@@ -261,11 +269,13 @@
     for i, (dy, dx) in enumerate(CHIPS):
         yy = lax.rem(y + sign * dy + NY, NY)
         xx = lax.rem(x + sign * dx + NX, NX)
-        value = acc[yy, xx]
-        for panel, (r, cf) in enumerate(((ra, ca), (rb, cb))):
-            if (panel, (dy, dx)) not in DONE:
-                value -= lax.dot_general(r[yy, xx], cf[...], NT, preferred_element_type=jnp.float32)
-        ob[i] = value.astype(jnp.bfloat16)
+        if (dy, dx) in READY:
+            product = acc[yy, xx]
+        else:
+            product = lax.dot_general(ra[yy, xx], ca[...], NT, preferred_element_type=jnp.float32)
+            product += lax.dot_general(rb[yy, xx], cb[...], NT, preferred_element_type=jnp.float32)
+        product = jnp.concatenate([product[:, k * LANES : k * LANES + CH] for k in range(NZ)], axis=1)
+        ob[i] = (tv[yy, xx].astype(jnp.float32) - product).astype(jnp.bfloat16)
         copy = pltpu.make_async_copy(ob.at[i], o_hbm.at[yy, xx], osem.at[i])
         copy.start()
         writes.append(copy)
@@ -280,26 +290,32 @@
     hbm = pl.BlockSpec(memory_space=pltpu.HBM)
     bf16 = jnp.bfloat16
     half = jax.ShapeDtypeStruct((NY, NX, PAIR, NB), bf16)
-    column = jax.ShapeDtypeStruct((COLS, NB), bf16)
+    column = jax.ShapeDtypeStruct((NZ * LANES, NB), bf16)
     blocks = (NY, NX, PAIR, COLS)
     inputs = (panel_block, diag_inverse, trailing.reshape(blocks))
     gathered = pl.pallas_call(
         gather_kernel,
         name="gather",
-        out_shape=[half, half, column, column, jax.ShapeDtypeStruct(blocks, jnp.float32)],
+        out_shape=[
+            half,
+            half,
+            column,
+            column,
+            jax.ShapeDtypeStruct((NY, NX, PAIR, NZ * LANES), jnp.float32),
+            jax.ShapeDtypeStruct(blocks, bf16),
+        ],
         in_specs=[hbm] * 3,
-        out_specs=[vmem] * 5,
+        out_specs=[vmem] * 6,
         scratch_shapes=[
             pltpu.VMEM((CH, 2 * NB), bf16),
             pltpu.VMEM((2, NB, NB), bf16),
-            pltpu.VMEM(blocks, bf16),
             pltpu.SemaphoreType.DMA((4,)),
             pltpu.SemaphoreType.DMA((N_SENDS,)),
             pltpu.SemaphoreType.DMA((64,)),
             pltpu.SemaphoreType.DMA((NZ * len(ZPARTS),)),
         ],
         compiler_params=pltpu.CompilerParams(
-            collective_id=0, has_side_effects=True, vmem_limit_bytes=24 << 20
+            collective_id=0, has_side_effects=True, vmem_limit_bytes=20 << 20
         ),
     )(*(pltpu.with_memory_space_constraint(a, pltpu.HBM) for a in inputs))
     factor, updated = pl.pallas_call(
@@ -316,7 +332,7 @@
             pltpu.SemaphoreType.DMA((NY * NX,)),
             pltpu.SemaphoreType.DMA((2,)),
         ],
-        compiler_params=pltpu.CompilerParams(vmem_limit_bytes=24 << 20),
+        compiler_params=pltpu.CompilerParams(vmem_limit_bytes=20 << 20),
     )(*gathered)
     return factor, updated.reshape(trailing.shape)
 

time: 42.8 us -> 41.8 us (0.977)
  Pallas kernels: 42 us -> 41 us
    pallas_call x1, Pallas kernels: 37.9 us -> 35.3 us  [body(): pl.pallas_call(gather_kernel, name='gather', out_shape=[half, half, colum...]
    pallas_call x1, Pallas kernels: 4.09 us -> 5.75 us  [body(): pl.pallas_call(update_kernel, name='update', out_shape=[jax.ShapeDtypeStr...]
where the time goes in v3:
time: 41.8 us; the launch traced here: 41.7 us
  Pallas kernels  41 us (98%)
  between operations  0.64 us (2%)
    pallas_call x1, Pallas kernels, body(): pl.pallas_call(gather_kernel, name='gather', out_shape=[half, half, colum...  35.3 us
    pallas_call x1, Pallas kernels, body(): pl.pallas_call(update_kernel, name='update', out_shape=[jax.ShapeDtypeStr...  5.75 us

profile of v3, /device:TPU:1, one launch (start us, length us, event | category | flops | bytes accessed | tf_op | source)
XLA Modules:
  0.0 41.7 jit_solution(7464815466699327683)
XLA Ops:
  0.6 35.3 %gather.1 = (bf16[4,4,224,512]{3,2,1,0:T(8,128)(2,1)S(1)}, bf16[4,4,224,512]{3,2,1,0:T(8,128)(2,1)S(1)}, bf16[1024,512]{1,0:T(8,128)(2,1)S(1)}, bf16[1024,512]{1...) custom-call(bf16[112,1024]{1,0:T(8,128)(2,1)} %panel_hbm.1, ...), custom_call_target="tpu_custom_call" | custom-call | tf_op jit(solution)/shard_map/gather/pallas_call | solution.py:296
  35.9 5.7 %update.1 = (bf16[112,1024]{1,0:T(8,128)(2,1)}, bf16[4,4,224,896]{3,2,1,0:T(8,128)(2,1)}) custom-call(bf16[4,4,224,512]{3,2,1,0:T(8,128)(2,1)S(1)} %get-tuple-element.10.ra, bf16[4,4,224,512]{3,2,1,0:T(8,128)(2,1)S(1)} %get-tuple-element.11.rb, bf16[1024,512]{1,0:T(8,128)(2,1)S(1)} %get-tuple-element.12.ca, bf16[1024,512]{1,0:T(8,128)(2,1)S(1)} %get-tuple-element.13.cb, ...), custom_call_target="tpu_custom_call" | custom-call | tf_op jit(solution)/shard_map/update/pallas_call | solution.py:321

commit v4 on v3

--- a/solution.py
+++ b/solution.py
@@ -13,7 +13,7 @@
 PAIR = 2 * CH
 COLS = NZ * CH
 ROWS = NY * NX * PAIR
-QUARTER = NB // 2
+WIDTH = NB
 LANES = 128
 TWO = 2 * LANES
 MESH = pl.DeviceIdType.MESH
@@ -29,43 +29,34 @@
     [(0, -1, 2), (1, 2, -1), (0, 2, 2), (1, 2, 2)],
     [(0, 2, 1), (1, 1, 2)],
 ]
-ZPARTS = [(0, 0), (0, QUARTER), (1, 0), (1, QUARTER)]
+ZPARTS = [(0, 0), (1, 0)]
 CROSS = [(0, 0), (0, -1), (0, 1), (-1, 0), (1, 0)]
 CORNERS = [(1, -1), (1, 1), (-1, -1), (-1, 1)]
 ENDS = [(0, 2), (2, 0)]
 PLAN = [
-    ("own", 3),
     ("z", 0, 1),
+    ("row", 0),
     ("z", 1, 1),
-    ("row", 0),
-    ("z", 2, 1),
-    ("z", 3, 1),
     ("row", 1),
     ("do", 1, CROSS),
     ("z", 0, 2),
+    ("row", 2),
     ("z", 1, 2),
-    ("row", 2),
-    ("z", 2, 2),
-    ("z", 3, 2),
     ("row", 3),
     ("do", 2, CROSS),
     ("z", 0, 3),
-    ("z", 1, 3),
     ("row", 4),
     ("do", 1, CORNERS),
-    ("z", 2, 3),
-    ("z", 3, 3),
+    ("z", 1, 3),
     ("do", 2, CORNERS),
     ("row", 5),
     ("do", 3, CROSS),
     ("do", 1, ENDS),
     ("do", 2, ENDS),
     ("z", 0, 4),
-    ("z", 1, 4),
     ("do", 3, CORNERS),
     ("row", 6),
-    ("z", 2, 4),
-    ("z", 3, 4),
+    ("z", 1, 4),
     ("do", 4, CROSS),
     ("row", 7),
     ("do", 3, ENDS),
@@ -178,7 +169,7 @@
     def zslot(part, dz):
         panel, first = ZPARTS[part]
         zz = lax.rem(z + sign * dz + NZ, NZ)
-        ref = cols[panel].at[pl.ds(pl.multiple_of(zz * LANES, LANES), CH), pl.ds(first, QUARTER)]
+        ref = cols[panel].at[pl.ds(pl.multiple_of(zz * LANES, LANES), CH), pl.ds(first, WIDTH)]
         return ref, zsem.at[part * NZ + zz]
 
     def zstart(part):
@@ -226,11 +217,10 @@
     pl.semaphore_wait(barrier, len(around))
     pass_on((0, 0, 0))
     zstart(0)
-    zstart(1)
     loads[2].wait()
     factor(1)
     pass_on((1, 0, 0))
-    zstart(2)
+    zstart(1)
     loads[3].start()
     for what, *arg in PLAN:
         if what == "row":
@@ -239,8 +229,6 @@
                 pass_on(chunk)
         elif what == "z":
             zpass_on(*arg)
-        elif what == "own":
-            zstart(*arg)
         else:
             update(*arg)
     for chunks in [[(0, 0, 0), (1, 0, 0)]] + RECV:

time: 41.8 us -> 41.5 us (level)
  no operation moved by 1% of the time
where the time goes in v4:
time: 41.5 us; the launch traced here: 41.4 us
  Pallas kernels  40.7 us (98%)
  between operations  0.64 us (2%)
    pallas_call x1, Pallas kernels, body(): pl.pallas_call(gather_kernel, name='gather', out_shape=[half, half, colum...  35 us
    pallas_call x1, Pallas kernels, body(): pl.pallas_call(update_kernel, name='update', out_shape=[jax.ShapeDtypeStr...  5.75 us

profile of v4, /device:TPU:1, one launch (start us, length us, event | category | flops | bytes accessed | tf_op | source)
XLA Modules:
  0.0 41.4 jit_solution(14731829757446146770)
XLA Ops:
  0.6 35.0 %gather.1 = (bf16[4,4,224,512]{3,2,1,0:T(8,128)(2,1)S(1)}, bf16[4,4,224,512]{3,2,1,0:T(8,128)(2,1)S(1)}, bf16[1024,512]{1,0:T(8,128)(2,1)S(1)}, bf16[1024,512]{1...) custom-call(bf16[112,1024]{1,0:T(8,128)(2,1)} %panel_hbm.1, ...), custom_call_target="tpu_custom_call" | custom-call | tf_op jit(solution)/shard_map/gather/pallas_call | solution.py:284
  35.6 5.8 %update.1 = (bf16[112,1024]{1,0:T(8,128)(2,1)}, bf16[4,4,224,896]{3,2,1,0:T(8,128)(2,1)}) custom-call(bf16[4,4,224,512]{3,2,1,0:T(8,128)(2,1)S(1)} %get-tuple-element.10.ra, bf16[4,4,224,512]{3,2,1,0:T(8,128)(2,1)S(1)} %get-tuple-element.11.rb, bf16[1024,512]{1,0:T(8,128)(2,1)S(1)} %get-tuple-element.12.ca, bf16[1024,512]{1,0:T(8,128)(2,1)S(1)} %get-tuple-element.13.cb, ...), custom_call_target="tpu_custom_call" | custom-call | tf_op jit(solution)/shard_map/update/pallas_call | solution.py:309
